TPU v7x, 32 devices: a whole 2x2x4 slice. The times are simulated.
32 devices in a mesh: dp: 8 (over z, y), sub: 4 (over x, core).
Axes of the slice: x: 2, y: 2, z: 4, core: 2. Of those that a mesh axis runs over, the one named last changes fastest.
Arguments:
- vectors: bfloat16 [16384, 1024], P(('dp', 'sub'))
- assignments: int32 [16384, 64], P('dp', 'sub'), may hold values from 0 to 255
- codebooks: float32 [64, 16, 256], replicated
Outputs:
- rotated: bfloat16 [16384, 1024], P('dp', 'sub')
- new_books: float32 [64, 16, 256], P('sub')
All inputs are finite; a program needn't handle non-finite values.
Results may differ from a plain program's by a relative error of at most 0.0044.
Values may be sent and summed in bfloat16 or wider, within the bound.
A program may use at most 64 MiB of HBM per device.

v0:
```python
import math

import jax
import jax.numpy as jnp
from jax import lax
from jax.sharding import PartitionSpec as P

NS_ITERS = 2


def newton_full(covariance, feature_count):
    iterate = (
        covariance * (math.sqrt(feature_count) / 3.0) / jnp.sqrt(jnp.sum(covariance * covariance))
    )
    for sweep in range(NS_ITERS):
        gram = lax.dot_general(
            iterate,
            iterate,
            (((0,), (0,)), ((), ())),
            precision=lax.Precision.HIGHEST,
            preferred_element_type=jnp.float32,
        )
        iterate = 1.5 * iterate - 0.5 * jnp.dot(
            iterate, gram, precision=lax.Precision.HIGHEST, preferred_element_type=jnp.float32
        )
    return iterate


def on_device(vectors, assignments, codebooks):
    row_count, feature_count = vectors.shape
    sub_total, sub_width, code_total = codebooks.shape
    own_subs = assignments.shape[1]
    row_codes = lax.all_to_all(assignments, "sub", split_axis=0, concat_axis=1, tiled=True)
    low_books = codebooks.astype(jnp.bfloat16)
    levels = jnp.arange(code_total, dtype=jnp.int32)
    block_rows = math.gcd(row_count, 512)
    block_count = row_count // block_rows

    def rebuild_block(block_codes):
        onehot = (block_codes[:, :, None] == levels[None, None, :]).astype(jnp.bfloat16)
        picked = lax.dot_general(
            onehot, low_books, (((2,), (2,)), ((1,), (0,))), preferred_element_type=jnp.float32
        )
        picked = jnp.transpose(picked, (1, 0, 2)).reshape(block_rows, feature_count)
        return picked.astype(jnp.bfloat16)

    rebuilt = lax.map(rebuild_block, row_codes.reshape(block_count, block_rows, sub_total)).reshape(
        row_count, feature_count
    )
    partial_value = lax.dot_general(
        vectors, rebuilt, (((0,), (0,)), ((), ())), preferred_element_type=jnp.float32
    )
    covariance = lax.psum(partial_value, ("dp", "sub"))
    rotation = newton_full(covariance, feature_count).astype(jnp.bfloat16)
    rotated = jnp.dot(vectors, rotation, preferred_element_type=jnp.float32).astype(jnp.bfloat16)
    owned_block = lax.all_to_all(rotated, "sub", split_axis=1, concat_axis=0, tiled=True)

    def per_subspace(subspace):
        column_block = lax.dynamic_slice_in_dim(owned_block, subspace * sub_width, sub_width, 1)
        code_column = lax.dynamic_slice_in_dim(assignments, subspace, 1, 1)
        onehot = (code_column == levels[None, :]).astype(jnp.bfloat16)
        code_sums = lax.dot_general(
            column_block, onehot, (((0,), (0,)), ((), ())), preferred_element_type=jnp.float32
        )
        counts = jnp.sum(onehot, axis=0, dtype=jnp.float32)
        return (code_sums, counts)

    code_sums, counts = lax.map(per_subspace, jnp.arange(own_subs, dtype=jnp.int32))
    code_sums, counts = lax.psum((code_sums, counts), "dp")
    old_books = lax.dynamic_slice_in_dim(codebooks, lax.axis_index("sub") * own_subs, own_subs, 0)
    new_books = jnp.where(
        counts[:, None, :] > 0, code_sums / jnp.maximum(counts, 1.0)[:, None, :], old_books
    )
    return (owned_block, new_books)


def solution(mesh):
    in_specs = (P(("dp", "sub"), None), P("dp", "sub"), P())
    out_specs = (P("dp", "sub"), P("sub", None, None))
    return jax.shard_map(
        on_device, mesh=mesh, in_specs=in_specs, out_specs=out_specs, check_vma=False
    )
```

profile of v0, /device:TPU:0, one launch (start us, length us, event | category | flops | bytes accessed | tf_op | source)
XLA Modules:
  0.0 463.0 jit_solution(15539860059312074080)
XLA Ops:
  8.2 8.6 %all_to_all.35 = s32[4,512,16]{1,2,0:T(8,128)S(1)} all-to-all(s32[4,512,16]{1,2,0:T(8,128)S(1)} %bitcast.49), channel_id=1, replica_groups=mesh['dp'=8,'sub'=4] {'sub'}, dimensions={0} | all-to-all | bytes 262144 | tf_op jit(solution)/shard_map/all_to_all | solution.py:33
  16.9 7.7 %fusion.11 = bf16[64,512,16]{1,2,0:T(8,128)(2,1)S(1)} fusion(s32[512,64]{0,1:T(8,128)S(1)} %bitcast.51, f32[64,16,256]{2,1,0:T(8,128)} %param.7), kind=kOutput, calls=%fused_computation.19 | convolution fusion | flops 277610496 | bytes 2228224 | tf_op jit(solution)/shard_map/while/body/eval_jaxpr/dot_general | solution.py:41
  24.6 3.3 convolution_bitcast_fusion
  27.8 142.8 %all-reduce.3.cloned.1.call-done = f32[1024,1024]{0,1:T(8,128)} async-done(((f32[1024,1024]{0,1:T(8,128)}), f32[1024,1024]{0,1:T(8,128)}) %all-reduce.3.cloned.1.call-update) | async-done | bytes 4194320 | tf_op jit(solution)/shard_map/psum | solution.py:53
  170.6 3.9 multiply_reduce_fusion
  175.2 18.1 %fusion.12 = f32[1024,1024]{1,0:T(8,128)S(1)} fusion(f32[1024,1024]{0,1:T(8,128)} %all-reduce.3.cloned.1.call-done, f32[]{:T(128)S(6)} %sqrt.3), kind=kOutput, calls=%fused_computation.21 | convolution fusion | flops 12886999040 | bytes 8388612 | tf_op jit(solution)/shard_map/dot_general | solution.py:16
  193.3 15.2 %multiply_subtract_fusion = f32[1024,1024]{0,1:T(8,128)S(1)} fusion(f32[1024,1024]{1,0:T(8,128)S(1)} %fusion.12, f32[]{:T(128)S(6)} %sqrt.3, f32[1024,1024]{0,1:T(8,128)S(1)} %copy-done.1), kind=kOutput, calls=%fused_computation.15 | convolution fusion | flops 12892241920 | bytes 12582916 | tf_op jit(solution)/shard_map/dot_general | solution.py:23
  208.5 14.3 %fusion.16 = f32[1024,1024]{1,0:T(8,128)S(1)} fusion(f32[1024,1024]{0,1:T(8,128)S(1)} %multiply_subtract_fusion), kind=kOutput, calls=%fused_computation.29 | convolution fusion | flops 12884901888 | bytes 8388608 | tf_op jit(solution)/shard_map/dot_general | solution.py:16
  222.8 14.3 %subtract_convert_fusion = bf16[1024,1024]{0,1:T(8,128)(2,1)S(1)} fusion(f32[1024,1024]{0,1:T(8,128)S(1)} %multiply_subtract_fusion, f32[1024,1024]{1,0:T(8,128)S(1)} %fusion.16), kind=kOutput, calls=%fused_computation.14 | convolution fusion | flops 12889096192 | bytes 10485760 | tf_op jit(solution)/shard_map/dot_general | solution.py:23
  237.1 2.3 convolution_convert_fusion
  239.4 3.5 all-to-all-start.1
  243.0 14.3 %all-to-all-done.1 = bf16[512,4,256]{0,2,1:T(8,128)(2,1)S(1)} async-done(((bf16[512,4,256]{0,2,1:T(8,128)(2,1)}), bf16[512,4,256]{0,2,1:T(8,128)(2,1)S(1)}, u32[]{:S(2)}, u32[]{:S(2)}) %all-to-all-start.1) | async-done | bytes 1048608 | tf_op jit(solution)/shard_map/all_to_all | solution.py:56
  257.8 93.6 %while.18 = (s32[]{:T(128)}, f32[16,16,256]{2,1,0:T(8,128)}, f32[16,256]{1,0:T(8,128)S(1)}, s32[16]{0:T(128)S(1)}, bf16[2048,256]{1,0:T(8,128)(2,1)S(1)}, /*index=5*/s32[2048,16]{0,1:T(8,128)}) while((s32[]{:T(128)}, f32[16,16,256]{2,1,0:T(8,128)}, f32[16,256]{1,0:T(8,128)S(1)}, s32[16]{0:T(128)S(1)}, ...), condition=%wide.region_4.5_spmd.clone.clone, body=%wide.region_2.4_spmd.clone.sunk.clone | while | flops 19398408 | bytes 577197 | solution.py:68
  261.9 1.4 fusion.31
  267.7 1.4 fusion.31
  273.6 1.4 fusion.31
  279.4 1.4 fusion.31
  285.3 1.4 fusion.31
  291.1 1.4 fusion.31
  297.0 1.4 fusion.31
  302.8 1.4 fusion.31
  308.7 1.4 fusion.31
  314.5 1.4 fusion.31
  320.4 1.4 fusion.31
  326.2 1.4 fusion.31
  332.1 1.4 fusion.31
  337.9 1.4 fusion.31
  343.8 1.4 fusion.31
  349.6 1.4 fusion.31
  351.5 35.2 %psum.22 = f32[16,256]{1,0:T(8,128)S(1)} all-reduce(f32[16,256]{1,0:T(8,128)S(1)} %get-tuple-element.55), channel_id=1, replica_groups=mesh['dp'=8,'sub'=4] {'dp'}, use_global_device_ids=true, to_apply=%region_5.6 | all-reduce | flops 4096 | bytes 32768 | tf_op jit(solution)/shard_map/psum | solution.py:69
  386.8 67.4 %all-reduce.5.cloned.1.call-done = f32[16,16,256]{2,1,0:T(8,128)} async-done(((f32[16,16,256]{2,1,0:T(8,128)}), f32[16,16,256]{2,1,0:T(8,128)}) %all-reduce.5.cloned.1.call-update) | async-done | bytes 262160 | tf_op jit(solution)/shard_map/psum | solution.py:69
  454.1 1.8 dynamic-slice_select_fusion
  (81 shorter events, 30.9 us)
Async XLA Ops:
  7.2 17.4 %copy-start = (bf16[512,1024]{1,0:T(8,128)(2,1)S(1)}, bf16[512,1024]{1,0:T(8,128)(2,1)}, u32[]{:S(2)}) copy-start(bf16[512,1024]{1,0:T(8,128)(2,1)} %param.5) | copy-start | bytes 3145732
  7.2 163.4 %all-reduce.3.cloned.1.call-start = ((), (), s32[]{:S(2)}) async-start(), calls=%async_computation.2 | async-start | bytes 8388608 | tf_op jit(solution)/shard_map/psum | solution.py:53
  175.2 18.1 %copy-start.1 = (f32[1024,1024]{0,1:T(8,128)S(1)}, f32[1024,1024]{0,1:T(8,128)}, u32[]{:S(2)}) copy-start(f32[1024,1024]{0,1:T(8,128)} %all-reduce.3.cloned.1.call-done) | copy-start | bytes 12582916
  239.4 17.9 %all-to-all-start.1 = ((bf16[512,4,256]{0,2,1:T(8,128)(2,1)}), bf16[512,4,256]{0,2,1:T(8,128)(2,1)S(1)}, u32[]{:S(2)}, u32[]{:S(2)}) async-start(bf16[512,4,256]{0,2,1:T(8,128)(2,1)} %bitcast.6), calls=%async_computation.1 | async-start | bytes 2097152 | tf_op jit(solution)/shard_map/all_to_all | solution.py:56
  242.9 211.2 %all-reduce.5.cloned.1.call-start = ((), (), s32[]{:S(2)}) async-start(), calls=%async_computation.3 | async-start | bytes 524288 | tf_op jit(solution)/shard_map/psum | solution.py:69
  351.5 104.5 %copy-start.2 = (bf16[2048,256]{1,0:T(8,128)(2,1)}, bf16[2048,256]{1,0:T(8,128)(2,1)S(1)}, u32[]{:S(2)}) copy-start(bf16[2048,256]{1,0:T(8,128)(2,1)S(1)} %get-tuple-element.161) | copy-start | bytes 3145732
Sparse Core Ops, SparseCore 0:
  28.0 142.6 all-reduce.2
  386.9 67.2 all-reduce.4
where the time goes:
time: 471 us; the launch traced here: 463 us
  waiting for transfers between devices  225 us (48%)
  matrix products  97.6 us (21%)
  blocking collectives  43.9 us (9%)
  loops' own time  41.9 us (9%)
  local copies, waits for them, and re-layouts  25.2 us (5%)
  between operations  15.1 us (3%)
  other arithmetic  11.3 us (2%)
    psum x1, waiting for transfers between devices, on_device(): covariance = lax.psum(partial_value, ('dp', 'sub'))  143 us
    psum x1, waiting for transfers between devices, on_device(): code_sums, counts = lax.psum((code_sums, counts), 'dp')  67.4 us
    another operation x1, loops' own time, on_device(): lax.map(per_subspace, jnp.arange(own_subs, dtype=jnp.int32))  41.9 us
    psum x1, blocking collectives, on_device(): code_sums, counts = lax.psum((code_sums, counts), 'dp')  35.2 us
    dot_general x2, matrix products, newton_full(): lax.dot_general(iterate, iterate, (((0,), (0,)), ((), ())), precision=lax...  32.4 us
    dot_general x2, matrix products, newton_full(): jnp.dot(iterate, gram, precision=lax.Precision.HIGHEST, preferred_element...  29.5 us
    dot_general x16, matrix products, per_subspace(): lax.dot_general(column_block, onehot, (((0,), (0,)), ((), ())), preferred...  22.5 us
    all_to_all x1, waiting for transfers between devices, on_device(): lax.all_to_all(rotated, 'sub', split_axis=1, concat_axis=0, tiled=True)  14.3 us
  transfers between devices with their start and end apart: 3, of which 3 were waited for; matrix products, arithmetic and copies ran while one was open for 0% of the time, Pallas kernels for 0%

commit v1 on v0

v1 whole, which is shorter than its diff:
```python
import functools
import math

import jax
import jax.numpy as jnp
from jax import lax
from jax.experimental import pallas as pl
from jax.experimental.pallas import tpu as pltpu
from jax.sharding import PartitionSpec as P

NS_ITERS = 2
MESH = pl.DeviceIdType.MESH
F32, BF16 = jnp.float32, jnp.bfloat16
NN = (((1,), (0,)), ((), ()))
NT = (((1,), (1,)), ((), ()))


def dot(a, b, dims=NN):
    return lax.dot_general(a, b, dims, preferred_element_type=F32)


def split_dot(a, b, dims=NN, passes=1):
    high = a.astype(BF16)
    out = dot(high, b, dims)
    if passes == 2:
        out = out + dot((a - high.astype(F32)).astype(BF16), b, dims)
    return out


def kernel(
    nd, chunks, passes,
    vec_ref, asg_ref, books_ref, rotated_ref, new_books_ref,
    gv, oh, rt, cpart, rsin, ct, cnt, cntin, sums, sumsin, means, zt, rott,
    own_sem, v_send, v_recv, n_send, n_recv, r_send, r_recv, a_send, a_recv,
    g_send, g_recv, s_send, s_recv, m_send, m_recv,
):
    d, s = lax.axis_index("dp"), lax.axis_index("sub")
    mate = s + 1 - 2 * (s % 2)
    across = (s + 2) % 4
    rows, feats = vec_ref.shape
    own_subs, total_rows = asg_ref.shape
    width, levels = books_ref.shape[1], books_ref.shape[2]
    cols = own_subs * width
    cw = feats // chunks
    row_groups = min(nd, 16)
    col_groups = nd // row_groups
    ph, pw = cols // row_groups, cw // col_groups
    sh = cols // nd

    barrier = pltpu.get_barrier_semaphore()
    for k in range(1, nd):
        pl.semaphore_signal(barrier, inc=1, device_id=((d + k) % nd, s), device_id_type=MESH)
    for peer in (mate, across):
        pl.semaphore_signal(barrier, inc=1, device_id=(d, peer), device_id_type=MESH)
    pl.semaphore_wait(barrier, nd + 1)

    pending = []

    def send(src, dst, send_sem, recv_sem, target):
        copy = pltpu.make_async_remote_copy(
            src_ref=src, dst_ref=dst, send_sem=send_sem, recv_sem=recv_sem,
            device_id=target, device_id_type=MESH,
        )
        copy.start()
        pending.append(copy)
        return copy

    def span(block, size):
        return pl.ds(pl.multiple_of(block * size, size), size)

    def strip(c):
        return pl.ds(c * cw, cw)

    own_rows = span(s, rows)
    own_copy = pltpu.make_async_copy(vec_ref, gv.at[own_rows], own_sem)
    own_copy.start()
    v_across, v_mate, v_pass = [], [], []
    for c in range(chunks):
        src = vec_ref.at[:, strip(c)]
        dst = gv.at[own_rows, strip(c)]
        v_across.append(send(src, dst, v_send.at[0, c], v_recv.at[0, c], (d, across)))
        v_mate.append(send(src, dst, v_send.at[1, c], v_recv.at[1, c], (d, mate)))

    def pass_vectors(c):
        v_across[c].wait_recv()
        block = gv.at[span(across, rows), strip(c)]
        v_pass.append(send(block, block, v_send.at[2, c], v_recv.at[2, c], (d, mate)))

    level = lax.broadcasted_iota(jnp.int32, (levels, 512), 0)
    ones = jnp.ones((16, total_rows), BF16)

    def build(m, carry):
        for b in range(total_rows // 512):
            code = asg_ref[pl.ds(m, 1), pl.ds(b * 512, 512)]
            oh[m, :, pl.ds(b * 512, 512)] = jnp.where(level == code, 1.0, 0.0).astype(BF16)
        book = books_ref[s * own_subs + m].astype(BF16)
        rt[span(m, width), :] = dot(book, oh[m]).astype(BF16)
        cnt[pl.ds(m, 1), :] = dot(ones, oh[m], NT)[0:1]
        return carry

    parts = 4
    for part in range(parts):
        step = own_subs // parts
        lax.fori_loop(part * step, (part + 1) * step, build, 0)
        if part % 2 == 1:
            pass_vectors(part // 2)
    n_copies = [
        send(cnt, cntin.at[k - 1], n_send.at[k - 1], n_recv.at[k - 1], ((d + k) % nd, s))
        for k in range(1, nd)
    ]
    own_copy.wait()

    def piece(q, c):
        r = pl.ds(pl.multiple_of((q % row_groups) * ph, ph), ph)
        w = pl.ds(pl.multiple_of(c * cw + (q // row_groups) * pw, pw), pw)
        return r, w

    def global_piece(q, c):
        r = pl.ds(pl.multiple_of(s * cols + (q % row_groups) * ph, ph), ph)
        return r, piece(q, c)[1]

    r_copies, a_copies, g_across, g_mate, g_pass = {}, {}, {}, {}, {}
    for t in range(chunks + 3):
        if t < chunks:
            for c in range(chunks):
                if c == len(v_pass) and c <= t + 1:
                    pass_vectors(c)
            v_mate[t].wait_recv()
            v_pass[t].wait_recv()
            cpart[:, strip(t)] = dot(rt[...], gv[:, strip(t)])
            for k in range(1, nd):
                q = (d + k) % nd
                r_copies[t, k] = send(
                    cpart.at[piece(q, t)], rsin.at[t, k - 1],
                    r_send.at[t, k - 1], r_recv.at[t, k - 1], (q, s),
                )
        c = t - 1
        if 0 <= c < chunks:
            total = cpart[piece(d, c)]
            for k in range(1, nd):
                r_copies[c, k].wait_recv()
                total = total + rsin[c, k - 1]
            ct[global_piece(d, c)] = total.astype(BF16)
            for k in range(1, nd):
                block = ct.at[global_piece(d, c)]
                a_copies[c, k] = send(
                    block, block, a_send.at[c, k - 1], a_recv.at[c, k - 1], ((d + k) % nd, s)
                )
        c = t - 2
        if 0 <= c < chunks:
            for k in range(1, nd):
                a_copies[c, k].wait_recv()
            block = ct.at[span(s, cols), strip(c)]
            g_across[c] = send(block, block, g_send.at[0, c], g_recv.at[0, c], (d, across))
            g_mate[c] = send(block, block, g_send.at[1, c], g_recv.at[1, c], (d, mate))
        c = t - 3
        if 0 <= c < chunks:
            g_across[c].wait_recv()
            block = ct.at[span(across, cols), strip(c)]
            g_pass[c] = send(block, block, g_send.at[2, c], g_recv.at[2, c], (d, mate))
    for c in range(chunks):
        g_mate[c].wait_recv()
        g_pass[c].wait_recv()

    square = jnp.zeros((8, feats), F32)
    for b in range(feats // 64):
        v = ct[pl.ds(b * 64, 64), :].astype(F32)
        square = square + jnp.sum((v * v).reshape(8, 8, feats), axis=0)
    norm = jnp.sum(square)
    scale = (math.sqrt(feats) / 3.0) / jnp.sqrt(jnp.full((1, feats), norm, F32))
    scale2 = scale * scale

    own = ct[span(s, cols), :]
    gram = dot(own, ct[...], NT) * scale2
    first = 1.5 * own.astype(F32) - 0.5 * split_dot(gram, ct[...], NN, passes)
    half = split_dot(first, ct[...], NT, passes) * scale2
    tail = split_dot(half, ct[...], NN, passes)
    gram1 = 1.5 * half - 0.5 * (split_dot(tail, ct[...], NT, passes) * scale2)
    prod = split_dot(gram1, ct[...], NN, passes)
    back = split_dot(prod, ct[...], NT, passes) * scale2
    second = 1.5 * first - 0.5 * (1.5 * prod - 0.5 * split_dot(back, ct[...], NN, passes))
    zt[...] = (second * scale).astype(BF16)

    for b in range(total_rows // 512):
        block = gv[pl.ds(b * 512, 512), :]
        rott[:, pl.ds(b * 512, 512)] = dot(zt[...], block, NT).astype(BF16)

    def accumulate(m, carry):
        sums[span(m, width), :] = dot(rott[span(m, width), :], oh[m], NT)
        return carry

    lax.fori_loop(0, own_subs, accumulate, 0)
    s_copies = []
    for k in range(1, nd):
        q = (d + k) % nd
        s_copies.append(
            send(sums.at[span(q, sh)], sumsin.at[k - 1], s_send.at[k - 1], s_recv.at[k - 1], (q, s))
        )
    for b in range(total_rows // 512):
        block = gv[pl.ds(b * 512, 512), :]
        rotated_ref[pl.ds(b * 512, 512), :] = dot(block, zt[...], NT).astype(BF16)
    counts = cnt[...]
    for k in range(1, nd):
        n_copies[k - 1].wait_recv()
        counts = counts + cntin[k - 1]
    total = sums[span(d, sh)]
    for k in range(1, nd):
        s_copies[k - 1].wait_recv()
        total = total + sumsin[k - 1]
    means[span(d, sh)] = total
    m_copies = []
    for k in range(1, nd):
        block = means.at[span(d, sh)]
        m_copies.append(
            send(block, block, m_send.at[k - 1], m_recv.at[k - 1], ((d + k) % nd, s))
        )
    for copy in m_copies:
        copy.wait_recv()
    for m in range(own_subs):
        n = counts[m:m + 1]
        value = means[pl.ds(m * width, width), :] / jnp.maximum(n, 1.0)
        new_books_ref[m] = jnp.where(n > 0, value, books_ref[s * own_subs + m])
    for copy in pending:
        copy.wait_send()


def on_device(nd, vectors, assignments, codebooks):
    rows, feats = vectors.shape
    total_rows, own_subs = assignments.shape
    width, levels = codebooks.shape[1:]
    cols = own_subs * width
    chunks = 4
    row_groups = min(nd, 16)
    ph, pw = cols // row_groups, feats // chunks // (nd // row_groups)
    sh = cols // nd
    dma = pltpu.SemaphoreType.DMA
    peers = nd - 1
    vmem = pl.BlockSpec(memory_space=pltpu.VMEM)
    return pl.pallas_call(
        functools.partial(kernel, nd, chunks, 1),
        out_shape=(
            jax.ShapeDtypeStruct((total_rows, cols), BF16),
            jax.ShapeDtypeStruct((own_subs, width, levels), F32),
        ),
        in_specs=[vmem] * 3,
        out_specs=(vmem, vmem),
        scratch_shapes=[
            pltpu.VMEM((total_rows, feats), BF16),
            pltpu.VMEM((own_subs, levels, total_rows), BF16),
            pltpu.VMEM((cols, total_rows), BF16),
            pltpu.VMEM((cols, feats), F32),
            pltpu.VMEM((chunks, peers, ph, pw), F32),
            pltpu.VMEM((feats, feats), BF16),
            pltpu.VMEM((own_subs, levels), F32),
            pltpu.VMEM((peers, own_subs, levels), F32),
            pltpu.VMEM((cols, levels), F32),
            pltpu.VMEM((peers, sh, levels), F32),
            pltpu.VMEM((cols, levels), F32),
            pltpu.VMEM((cols, feats), BF16),
            pltpu.VMEM((cols, total_rows), BF16),
            dma,
            dma((3, chunks)), dma((3, chunks)),
            dma((peers,)), dma((peers,)),
            dma((chunks, peers)), dma((chunks, peers)),
            dma((chunks, peers)), dma((chunks, peers)),
            dma((3, chunks)), dma((3, chunks)),
            dma((peers,)), dma((peers,)),
            dma((peers,)), dma((peers,)),
        ],
        compiler_params=pltpu.CompilerParams(
            collective_id=0, has_side_effects=True, vmem_limit_bytes=58 * 1024 * 1024
        ),
    )(vectors, assignments.T, codebooks)


def solution(mesh):
    in_specs = (P(("dp", "sub"), None), P("dp", "sub"), P())
    out_specs = (P("dp", "sub"), P("sub", None, None))
    return jax.shard_map(
        functools.partial(on_device, mesh.shape["dp"]),
        mesh=mesh, in_specs=in_specs, out_specs=out_specs, check_vma=False,
    )
```

time: 471 us -> 96.2 us (0.20); the launches traced: 463 us -> 95.7 us
  waiting for transfers between devices: 225 us -> 0 us
  matrix products: 97.6 us -> 0 us
  Pallas kernels: 0 us -> 92 us
  blocking collectives: 43.9 us -> 0 us
  loops' own time: 41.9 us -> 0 us
  local copies, waits for them, and re-layouts: 25.2 us -> 3.01 us
  between operations: 15.1 us -> 0.65 us
  other arithmetic: 11.3 us -> 0 us
    psum x2 -> x0, waiting for transfers between devices: 210 us -> none  [the longest x1 143 us: on_device(): covariance = lax.psum(partial_value, ('dp', 'sub'))]
    dot_general x23 -> x0, matrix products: 97.6 us -> none  [the longest x2 32.4 us: newton_full(): lax.dot_general(iterate, iterate, (((0,), (0,)), ((), ())), precision=lax...]
    pallas_call x0 -> x1, Pallas kernels: none -> 92 us  [on_device(): pl.pallas_call(functools.partial(kernel, nd, chunks, 1), out_shape=(jax.S...]
    another operation x1 -> x0, loops' own time: 41.9 us -> none  [on_device(): lax.map(per_subspace, jnp.arange(own_subs, dtype=jnp.int32))]
    psum x1 -> x0, blocking collectives: 35.2 us -> none  [on_device(): code_sums, counts = lax.psum((code_sums, counts), 'dp')]
    dynamic_slice x32 -> x0, local copies, waits for them, and re-layouts: 23 us -> none  [the longest x16 13.6 us: per_subspace(): code_column = lax.dynamic_slice_in_dim(assignments, subspace, 1, 1)]
    all_to_all x1 -> x0, waiting for transfers between devices: 14.3 us -> none  [on_device(): lax.all_to_all(rotated, 'sub', split_axis=1, concat_axis=0, tiled=True)]
    reduce_sum x17 -> x0, other arithmetic: 9.46 us -> none  [the longest x16 5.59 us: per_subspace(): counts = jnp.sum(onehot, axis=0, dtype=jnp.float32)]
  transfers between devices with their start and end apart: 3 -> 0, of which waited for: 3 -> 0; matrix products, arithmetic and copies ran while one was open for 0% -> 0% of each run, Pallas kernels for 0% -> 0%
where the time goes in v1:
time: 96.2 us; the launch traced here: 95.7 us
  Pallas kernels  92 us (96%)
  local copies, waits for them, and re-layouts  3.01 us (3%)
    pallas_call x1, Pallas kernels, on_device(): pl.pallas_call(functools.partial(kernel, nd, chunks, 1), out_shape=(jax.S...  92 us
    unnamed x4, local copies, waits for them, and re-layouts  3.01 us

profile of v1, /device:TPU:0, one launch (start us, length us, event | category | flops | bytes accessed | tf_op | source)
XLA Modules:
  0.0 95.7 jit_solution(1811728138287327036)
XLA Ops:
  0.6 92.0 %shard_map.50 = (bf16[2048,256]{1,0:T(8,128)(2,1)}, f32[16,16,256]{2,1,0:T(8,128)}) custom-call(bf16[512,1024]{1,0:T(8,128)(2,1)} %vec_ref.1, s32[16,2048]{1,0:T(8,128)} %bitcast.1, f32[64,16,256]{2,1,0:T(8,128)} %books_ref.1), custom_call_target="tpu_custom_call" | custom-call | tf_op jit(solution)/shard_map/pallas_call | solution.py:239
  92.7 0.0 copy-start
  92.7 2.3 %copy.7 = bf16[2048,256]{1,0:T(8,128)(2,1)} copy(bf16[2048,256]{1,0:T(8,128)(2,1)} %get-tuple-element.4) | data formatting | bytes 2097152
  95.0 0.0 copy-done
  95.0 0.7 copy.8
Async XLA Ops:
  92.7 2.3 %copy-start = (f32[16,16,256]{2,1,0:T(8,128)S(1)}, f32[16,16,256]{2,1,0:T(8,128)}, u32[]{:S(2)}) copy-start(f32[16,16,256]{2,1,0:T(8,128)} %get-tuple-element.5) | copy-start | bytes 786436
